TPU v7x, 256 devices: a whole 4x4x8 slice. The times are simulated.
256 devices in a mesh: cluster: 16 (over y_hi, z), client: 16 (over x, y_lo, core).
Axes of the slice: x: 4, y: 4 (y_hi: 2, y_lo: 2; y = y_hi * 2 + y_lo), z: 8, core: 2. Of those that a mesh axis runs over, the one named last changes fastest.
Arguments:
- user_feats: bfloat16 [24576, 2048], P('client'), may hold values from -6 to 6
- item_feats: bfloat16 [24576, 2048], P('client'), may hold values from -6 to 6
- item_ids: int32 [24576], P('client'), may hold values from 0 to 999
- picks: int32 [256], P('client'), may hold values from 0 to 15
- user_weight: bfloat16 [16, 2048, 512], P('cluster'), may hold values from -0.125 to 0.125
- item_weight: bfloat16 [16, 2048, 512], P('cluster'), may hold values from -0.125 to 0.125
Outputs:
- loss_table: float32 [256, 16], P('client')
- user_grad: float32 [16, 2048, 512], P('cluster', 'client')
- item_grad: float32 [16, 2048, 512], P('cluster', 'client')
Inputs may be any that keep to these rules, and one draw needn't show every extreme that they name: `picks`: one cluster per client.
All inputs are finite; a program needn't handle non-finite values.
Results may differ from a plain program's by a relative error of at most 0.005.
Values sent between devices are 32-bit elements; how exact they have to be, the bound alone decides.
A program may use at most 128 MiB of HBM per device.

v0:
```python
import math

import jax
import jax.numpy as jnp
from jax import lax
from jax.sharding import Mesh
from jax.sharding import PartitionSpec as P

CLUSTER = ("cluster_0", "cluster_1")


def joined_along(blocks, dim):
    blocks = jnp.moveaxis(blocks, 0, dim)
    dims = blocks.shape
    return blocks.reshape(*dims[:dim], dims[dim] * dims[dim + 1], *dims[dim + 2 :])


def gather_in_order(x, axes, turns):
    blocks = x
    for k in turns:
        blocks = lax.all_gather(blocks, axes[k])
    done = turns[::-1]
    back = [done.index(k) for k in range(len(axes))]
    blocks = blocks.transpose(*back, *range(len(axes), blocks.ndim))
    return blocks.reshape(-1, *x.shape)


def gather_axes(x, axes, turns, dim):
    return joined_along(gather_in_order(x, axes, turns), dim)


def silu_slope(pre_act):
    sig = jax.nn.sigmoid(pre_act)
    return sig * (1.0 + pre_act * (1.0 - sig))


def contract_rows(left, right):
    return lax.dot_general(
        left, right, (((0,), (0,)), ((), ())), preferred_element_type=jnp.float32
    )


def body(user_feats, item_feats, item_ids, picks, user_weight, item_weight):
    cluster_index = lax.axis_index(CLUSTER)
    user_map = user_weight[0]
    item_map = item_weight[0]
    clients = picks.shape[0]
    row_count = user_feats.shape[0]
    per_client = row_count // clients
    width = user_map.shape[1]
    temper = 1.0 / math.sqrt(width)
    pre_user = jnp.dot(user_feats, user_map, preferred_element_type=jnp.float32)
    user_vec = jax.nn.silu(pre_user).astype(jnp.bfloat16)
    item_vec = jnp.dot(item_feats, item_map, preferred_element_type=jnp.float32).astype(
        jnp.bfloat16
    )
    user_blocks = user_vec.reshape(clients, per_client, width)
    item_blocks = item_vec.reshape(clients, per_client, width)
    scores = (
        jnp.einsum("cre,cte->crt", user_blocks, item_blocks, preferred_element_type=jnp.float32)
        * temper
    )
    grouped = item_ids.reshape(clients, per_client)
    labels = (grouped[:, :, None] == grouped[:, None, :]).astype(jnp.float32)
    pair_loss = jax.nn.softplus(scores) - labels * scores
    client_loss = jnp.mean(pair_loss, axis=(1, 2))
    loss_table = gather_axes(client_loss[:, None], CLUSTER, (0, 1), 1)
    chosen = (picks == cluster_index).astype(jnp.float32)
    slope = ((jax.nn.sigmoid(scores) - labels) * temper * chosen[:, None, None]).astype(
        jnp.bfloat16
    )
    user_slope = jnp.einsum(
        "crt,cte->cre", slope, item_blocks, preferred_element_type=jnp.float32
    ).reshape(row_count, width)
    pre_slope = (user_slope * silu_slope(pre_user)).astype(jnp.bfloat16)
    item_slope = (
        jnp.einsum("crt,cre->cte", slope, user_blocks, preferred_element_type=jnp.float32)
        .reshape(row_count, width)
        .astype(jnp.bfloat16)
    )
    partial_sum = lax.psum_scatter(
        jnp.concatenate(
            [contract_rows(user_feats, pre_slope), contract_rows(item_feats, item_slope)], axis=1
        ),
        "client",
        scatter_dimension=0,
        tiled=True,
    )
    return (loss_table, partial_sum[None, :, :width], partial_sum[None, :, width:])


def solution(mesh):
    split = Mesh(
        mesh.devices.reshape(2, 8, mesh.shape["client"]), ("cluster_0", "cluster_1", "client")
    )
    in_specs = (
        P("client", None),
        P("client", None),
        P("client"),
        P("client"),
        P(CLUSTER, None, None),
        P(CLUSTER, None, None),
    )
    out_specs = (P("client", None), P(CLUSTER, "client", None), P(CLUSTER, "client", None))
    return jax.shard_map(body, mesh=split, in_specs=in_specs, out_specs=out_specs, check_vma=False)
```

profile of v0, /device:TPU:1, one launch (start us, length us, event | category | flops | bytes accessed | tf_op | source)
XLA Modules:
  0.0 147.6 jit_solution(15566198637348806713)
XLA Ops:
  7.2 0.0 copy-start
  7.2 0.0 reduce-scatter.2.cloned.1.call-start
  7.2 0.9 eq.21
  8.1 0.7 compare_select_fusion.1
  8.8 0.0 copy-start.1
  8.8 7.0 %convolution_convert_fusion = bf16[1536,512]{1,0:T(8,128)(2,1)S(1)} fusion(bf16[1536,2048]{1,0:T(8,128)(2,1)} %param.7, bf16[1,2048,512]{2,1,0:T(8,128)(2,1)} %param.11), kind=kOutput, calls=%fused_computation.7 | convolution fusion | flops 3222011904 | bytes 9961472 | tf_op jit(solution)/shard_map/dot_general | solution.py:54
  15.8 0.0 copy-done
  15.8 0.0 copy-done.1
  15.8 3.9 %multiply_convert_fusion = (bf16[1536,512]{1,0:T(8,128)(2,1)S(1)}, f32[1536,512]{1,0:T(8,128)S(1)}) fusion(bf16[1536,2048]{1,0:T(8,128)(2,1)S(1)} %copy-done.1, bf16[1,2048,512]{2,1,0:T(8,128)(2,1)S(1)} %copy-done), kind=kOutput, calls=%fused_computation.5 | convolution fusion | flops 3225157632 | bytes 13107200 | tf_op jit(solution)/shard_map/dot_general | solution.py:52
  19.7 0.6 fusion.9
  20.3 1.1 convolution_convert_fusion.1
  21.4 1.1 fusion.11
  22.4 0.0 slice-start
  22.5 1.1 fusion
  23.6 0.0 slice-start.1
  23.6 3.5 %convolution_bitcast_fusion.1 = f32[2048,512]{0,1:T(8,128)S(1)} fusion(bf16[1536,512]{1,0:T(8,128)(2,1)S(1)} %fusion, bf16[1536,2048]{1,0:T(8,128)(2,1)S(1)} %copy-done.1), kind=kOutput, calls=%fused_computation.2 | convolution fusion | flops 3221225472 | bytes 12058624 | tf_op jit(solution)/shard_map/dot_general | solution.py:38
  27.1 0.0 slice-done
  27.1 0.0 slice-done.1
  27.1 3.5 %convolution_bitcast_fusion = f32[2048,512]{0,1:T(8,128)S(1)} fusion(bf16[1536,512]{1,0:T(8,128)(2,1)S(1)} %bitcast.54, bf16[1536,2048]{1,0:T(8,128)(2,1)S(1)} %bitcast.53), kind=kOutput, calls=%fused_computation.1 | convolution fusion | flops 3221225472 | bytes 12058624 | tf_op jit(solution)/shard_map/dot_general | solution.py:38
  30.6 3.8 %pad_maximum_fusion = f32[2048,1024]{0,1:T(8,128)} fusion(f32[2048,512]{0,1:T(8,128)S(1)} %convolution_bitcast_fusion, f32[2048,512]{0,1:T(8,128)S(1)} %convolution_bitcast_fusion.1), kind=kLoop, calls=%fused_computation | loop fusion | flops 2097152 | bytes 16777216 | tf_op jit(solution)/shard_map/concatenate | solution.py:82
  34.4 0.0 copy-start.2
  34.4 0.0 reduce-scatter.2.cloned.1.call-update
  34.4 0.6 copy-done.2
  35.0 0.6 dynamic-slice
  36.3 0.7 fusion.5
  37.0 0.1 multiply_dynamic-update-slice_fusion
  37.1 6.0 %all-reduce = f32[32]{0:T(128)S(1)} all-reduce(f32[32]{0:T(128)S(1)} %multiply_dynamic-update-slice_fusion), channel_id=2, replica_groups=mesh['cluster_0'=2,'cluster_1'=8,'client'=16] {'cluster_0'}, use_global_device_ids=true, to_apply=%add | all-reduce | flops 32 | bytes 256
  43.1 0.1 reshape.40
  43.2 16.6 %all-gather.1 = f32[16,16,1]{1,2,0:T(1,128)S(1)} all-gather(f32[2,16,1]{1,2,0:T(1,128)S(1)} %bitcast.51), channel_id=3, replica_groups=mesh['cluster_0'=2,'cluster_1'=8,'client'=16] {'cluster_1'}, dimensions={0}, use_global_device_ids=true | all-gather | bytes 1152 | tf_op jit(solution)/shard_map/all_gather | solution.py:21
  59.7 0.7 copy.26
  60.4 77.6 %reduce-scatter.2.cloned.1.call-done = f32[128,1024]{0,1:T(8,128)} async-done(((f32[2048,1024]{0,1:T(8,128)}), f32[128,1024]{0,1:T(8,128)}) %reduce-scatter.2.cloned.1.call-update) | async-done | bytes 524304 | tf_op jit(solution)/shard_map/reduce_scatter | solution.py:81
  138.0 1.1 slice_bitcast_fusion
  139.1 0.8 copy.28
  139.9 0.8 copy.27
  (3 shorter events, 0.0 us)
Async XLA Ops:
  7.2 8.6 %copy-start = (bf16[1,2048,512]{2,1,0:T(8,128)(2,1)S(1)}, bf16[1,2048,512]{2,1,0:T(8,128)(2,1)}, u32[]{:S(2)}) copy-start(bf16[1,2048,512]{2,1,0:T(8,128)(2,1)} %param.10) | copy-start | bytes 6291460
  7.2 130.8 %reduce-scatter.2.cloned.1.call-start = ((), (), s32[]{:S(2)}) async-start(), calls=%async_computation.1 | async-start | bytes 8912896 | tf_op jit(solution)/shard_map/reduce_scatter | solution.py:81
  8.8 7.0 %copy-start.1 = (bf16[1536,2048]{1,0:T(8,128)(2,1)S(1)}, bf16[1536,2048]{1,0:T(8,128)(2,1)}, u32[]{:S(2)}) copy-start(bf16[1536,2048]{1,0:T(8,128)(2,1)} %param.6) | copy-start | bytes 18874372
  22.4 4.6 %slice-start = ((s8[6291456]{0:T(1024)(128)(4,1)}), s8[2097152]{0:T(1024)(128)(4,1)S(1)}, s32[]{:S(2)}) async-start(s8[6291456]{0:T(1024)(128)(4,1)} %bitcast.52), calls=%async_computation.2 | async-start | bytes 4194304
  23.6 3.5 %slice-start.1 = ((s8[6291456]{0:T(1024)(128)(4,1)}), s8[4194304]{0:T(1024)(128)(4,1)S(1)}, s32[]{:S(2)}) async-start(s8[6291456]{0:T(1024)(128)(4,1)} %bitcast.52), calls=%async_computation.3 | async-start | bytes 8388608
  34.4 0.7 copy-start.2
Sparse Core Ops, SparseCore 0:
  34.5 103.4 reduce-scatter.1
where the time goes:
time: 148 us
  waiting for transfers between devices  77.6 us (52%)
  blocking collectives  22.6 us (15%)
  matrix products  20.5 us (14%)
  between operations  14.8 us (10%)
  other arithmetic  6.34 us (4%)
  local copies, waits for them, and re-layouts  5.66 us (4%)
    reduce_scatter x1, waiting for transfers between devices, body(): lax.psum_scatter(jnp.concatenate([contract_rows(user_feats, pre_slope), c...  77.6 us
    all_gather x1, blocking collectives, gather_in_order(): blocks = lax.all_gather(blocks, axes[k])  16.6 us
    dot_general x1, matrix products, body(): jnp.dot(item_feats, item_map, preferred_element_type=jnp.float32)  6.99 us
    dot_general x2, matrix products, contract_rows(): lax.dot_general(left, right, (((0,), (0,)), ((), ())), preferred_element_...  6.94 us
    unnamed x1, blocking collectives  6.02 us
    dot_general x1, matrix products, body(): pre_user = jnp.dot(user_feats, user_map, preferred_element_type=jnp.float32)  3.86 us
    concatenate x1, other arithmetic, body(): jnp.concatenate([contract_rows(user_feats, pre_slope), contract_rows(item...  3.79 us
    unnamed x15, local copies, waits for them, and re-layouts  3.6 us
  transfers between devices with their start and end apart: 1, of which 1 were waited for; matrix products, arithmetic and copies ran while one was open for 1% of the time, Pallas kernels for 0%

commit v1 on v0

v1 whole, which is shorter than its diff:
```python
import functools
import math

import jax
import jax.numpy as jnp
from jax import lax
from jax.experimental import pallas as pl
from jax.experimental.pallas import tpu as pltpu
from jax.sharding import PartitionSpec as P

MESH = pl.DeviceIdType.MESH
NX = 4
ORDER = (2, 1, 3, 0)


def kernel(cfg, uf, itf, ids, picks, uw, iw, loss_out, ug_out, ig_out,
           fu, fi, wu, wi, pre, iv, uvec, pst, ist, gt, crecv, ya, yb,
           xa1, xal, xar, xb1, xbl, xbr, tile, table,
           ld, cs, cr, ys, yr, xs, xr, ls, lr):
    clients, rows, width, split, groups, clusters = cfg
    depth = fu.shape[1]
    per = clients // groups
    grp = per * rows
    temper = 1.0 / math.sqrt(width)
    k_me = lax.axis_index("cluster")
    s_me = lax.axis_index("client")
    x = s_me // 4
    y = (s_me // 2) % 2
    c = s_me % 2
    mate = {"client": x * 4 + y * 2 + (1 - c)}
    across = {"client": x * 4 + (1 - y) * 2 + c}
    right = {"client": ((x + 1) % NX) * 4 + y * 2 + c}
    left = {"client": ((x + NX - 1) % NX) * 4 + y * 2 + c}

    def load(src, dst, n):
        return pltpu.make_async_copy(src, dst, ld.at[n])

    load_wu = load(uw.at[0], wu, 0)
    load_wi = load(iw.at[0], wi, 1)
    load_u = [load(uf.at[pl.ds(g * grp, grp)], fu.at[pl.ds(g * grp, grp)], 2 + g) for g in range(groups)]
    load_i = [load(itf.at[pl.ds(g * grp, grp)], fi.at[pl.ds(g * grp, grp)], 2 + groups + g) for g in range(groups)]
    load_wu.start()
    load_u[0].start()
    load_wi.start()
    load_i[0].start()
    for g in range(1, groups):
        load_u[g].start()
        load_i[g].start()

    barrier = pltpu.get_barrier_semaphore()
    for peer in (mate, across, right, left):
        pl.semaphore_signal(barrier, inc=1, device_id=peer, device_id_type=MESH)
    for n in range(1, clusters):
        pl.semaphore_signal(barrier, inc=1, device_id={"cluster": (k_me + n) % clusters}, device_id_type=MESH)

    def towers(g):
        if g == 0:
            load_wu.wait()
        load_u[g].wait()
        pre[g % 2] = jnp.dot(fu[g * grp:(g + 1) * grp, :], wu[...], preferred_element_type=jnp.float32)
        if g == 0:
            load_wi.wait()
        load_i[g].wait()
        iv[g % 2] = jnp.dot(fi[g * grp:(g + 1) * grp, :], wi[...], preferred_element_type=jnp.float32).astype(jnp.bfloat16)

    def slopes(g):
        p = pre[g % 2]
        sig = 1.0 / (1.0 + jnp.exp(-p))
        uvec[...] = (p * sig).astype(jnp.bfloat16)
        pre[g % 2] = sig * (1.0 + p * (1.0 - sig))
        pres, items = [], []
        for n in range(per):
            client = g * per + n
            at = slice(n * rows, (n + 1) * rows)
            u = uvec[at, :]
            v = iv[g % 2, at, :]
            s = lax.dot_general(u, v, (((1,), (1,)), ((), ())), preferred_element_type=jnp.float32) * temper
            across_ids = jnp.broadcast_to(ids[pl.ds(client, 1), :], (rows, rows))
            labels = (across_ids == across_ids.T).astype(jnp.float32)
            tail = jnp.exp(-jnp.abs(s))
            pair = jnp.maximum(s, 0.0) + jnp.log(1.0 + tail) - labels * s
            mean = jnp.sum(pair, axis=(0, 1), keepdims=True) / (rows * rows)
            tile[pl.ds(client, 1), :] = jnp.broadcast_to(mean, (1, 128))
            gate = jnp.where(s >= 0.0, 1.0, tail) / (1.0 + tail)
            chosen = jnp.where(picks[client] == k_me, temper, 0.0).astype(jnp.float32)
            slope = ((gate - labels) * chosen).astype(jnp.bfloat16)
            us = jnp.dot(slope, v, preferred_element_type=jnp.float32)
            pres.append(us * pre[g % 2, at, :])
            items.append(lax.dot_general(slope, u, (((0,), (0,)), ((), ())), preferred_element_type=jnp.float32))
        pst[:, g * grp:(g + 1) * grp] = jnp.concatenate(pres, axis=0).T.astype(jnp.bfloat16)
        ist[:, g * grp:(g + 1) * grp] = jnp.concatenate(items, axis=0).T.astype(jnp.bfloat16)

    towers(0)
    for g in range(groups):
        if g + 1 < groups:
            towers(g + 1)
        slopes(g)

    pl.semaphore_wait(barrier, 4 + clusters - 1)

    table[pl.ds(k_me, 1)] = tile[...][None]
    loss_copies = []
    for n in range(1, clusters):
        copy = pltpu.make_async_remote_copy(
            src_ref=tile, dst_ref=table.at[k_me], send_sem=ls.at[n], recv_sem=lr.at[n],
            device_id={"cluster": (k_me + n) % clusters}, device_id_type=MESH)
        copy.start()
        loss_copies.append(copy)

    A = pl.ds(0, split)
    B = pl.ds(split, width - split)

    def step_of(dx, dy):
        return 2 * ORDER.index(dx) + (1 - dy)

    def own(dx, dy, t, part):
        return gt.at[step_of(dx, dy), t, c, part]

    def send(src, dst, ssem, rsem, peer):
        return pltpu.make_async_remote_copy(src_ref=src, dst_ref=dst, send_sem=ssem, recv_sem=rsem,
                                            device_id=peer, device_id_type=MESH)

    def core_copy(step, t):
        return send(gt.at[step, t, 1 - c], crecv.at[step, t], cs.at[step, t], cr.at[step, t], mate)

    def ya_copy(dx, t):
        return send(own(dx, 1, t, A), ya.at[dx, t], ys.at[dx, t], yr.at[dx, t], across)

    def yb_copy(t):
        return send(own(0, 1, t, B), yb.at[t], ys.at[4, t], yr.at[4, t], across)

    def x_part(which):
        return (0, A, xa1, xal, xar) if which == 2 else (which, B, xb1.at[which], xbl.at[which], xbr.at[which])

    def far_copy(which, t):
        dy, part, first, _, _ = x_part(which)
        return send(own(2, dy, t, part), first.at[t], xs.at[which, 0, t], xr.at[which, 0, t], (right, left)[t])

    def near_copy(which, t, rightward):
        dy, part, _, from_left, from_right = x_part(which)
        if rightward:
            return send(own(1, dy, t, part), from_left.at[t], xs.at[which, 1, t], xr.at[which, 1, t], right)
        return send(own(3, dy, t, part), from_right.at[t], xs.at[which, 2, t], xr.at[which, 2, t], left)

    def add(dst, src):
        dst[...] += src[...]

    def far_arrived(which, t):
        dy, part, first, _, _ = x_part(which)
        far_copy(which, t).wait_recv()
        add(own((1, 3)[t], dy, t, part), first.at[t])
        near_copy(which, t, t == 0).start()

    def near_arrived(which):
        dy, part, _, from_left, from_right = x_part(which)
        for t in (0, 1):
            near_copy(which, t, True).wait_recv()
            near_copy(which, t, False).wait_recv()
            mine = own(0, dy, t, part)
            mine[...] += from_left[t] + from_right[t]

    def ya_arrived(dx):
        for t in (0, 1):
            ya_copy(dx, t).wait_recv()
            add(own(dx, 0, t, A), ya.at[dx, t])

    def ready(step):
        dx, dy = ORDER[step // 2], 1 - step % 2
        for t in (0, 1):
            core_copy(step, t).wait_recv()
            mine = gt.at[step, t, c]
            mine[...] += crecv[step, t]
            if dx == 2:
                far_copy(dy, t).start()
            if dy == 1:
                ya_copy(dx, t).start()
            if dx == 1 and t == 1:
                near_copy(dy, 1, True).start()
            if dx == 3 and t == 0:
                near_copy(dy, 0, False).start()

    def body(step, carry):
        q = step // 2
        dx = (2 + 3 * q + 3 * (q * (q - 1) // 2)) % NX
        dy = 1 - step % 2
        chip = ((x + dx) % NX) * 2 + (y + dy) % 2
        cols = pl.ds(pl.multiple_of(chip * 256, 256), 256)
        for t, (left_t, feats) in enumerate(((pst, fu), (ist, fi))):
            r = jnp.dot(left_t[...], feats[:, cols], preferred_element_type=jnp.float32)
            gt[step, t, 0] = r[:, :128]
            gt[step, t, 1] = r[:, 128:]
            core_copy(step, t).start()
        for n in range(2 * NX - 1):
            @pl.when(step == n + 1)
            def _(n=n):
                ready(n)
                if n >= 3:
                    far_arrived(n % 2, (n - 3) // 2)
        return carry

    lax.fori_loop(0, 2 * NX, body, 0)
    ready(2 * NX - 1)
    ya_arrived(2)
    far_copy(2, 0).start()
    far_copy(2, 1).start()
    ya_arrived(1)
    near_copy(2, 1, True).start()
    ya_arrived(3)
    near_copy(2, 0, False).start()
    near_arrived(1)
    yb_copy(0).start()
    yb_copy(1).start()
    far_arrived(2, 0)
    far_arrived(2, 1)
    near_arrived(0)
    ya_arrived(0)

    for copy in loss_copies:
        copy.wait()
    lane = lax.broadcasted_iota(jnp.int32, (clients, 128), 1)
    total = jnp.zeros((clients, 128), jnp.float32)
    for n in range(clusters):
        total = total + jnp.where(lane == n, table[n], 0.0)
    loss_out[...] = total[:, :clusters]

    outs = (ug_out, ig_out)
    for t in (0, 1):
        yb_copy(t).wait_recv()
        res = gt[step_of(0, 0), t, c, split:, :] + yb[t]
        outs[t][0, :, split:] = res.T
    near_arrived(2)
    for t in (0, 1):
        outs[t][0, :, :split] = gt[step_of(0, 0), t, c, :split, :].T

    for step in range(2 * NX):
        for t in (0, 1):
            core_copy(step, t).wait_send()
    for t in (0, 1):
        for dx in range(NX):
            ya_copy(dx, t).wait_send()
        yb_copy(t).wait_send()
        for which in range(3):
            far_copy(which, t).wait_send()
            near_copy(which, t, True).wait_send()
            near_copy(which, t, False).wait_send()


def body(user_feats, item_feats, item_ids, picks, user_weight, item_weight):
    clients = picks.shape[0]
    total, depth = user_feats.shape
    rows = total // clients
    width = user_weight.shape[2]
    clusters = lax.axis_size("cluster")
    groups = 4
    grp = total // groups
    split = width * 7 // 16
    rest = width - split
    f32, bf16 = jnp.float32, jnp.bfloat16
    vmem = pltpu.VMEM
    dma = pltpu.SemaphoreType.DMA
    any_spec = pl.BlockSpec(memory_space=pl.ANY)
    vmem_spec = pl.BlockSpec(memory_space=pltpu.VMEM)
    smem_spec = pl.BlockSpec(memory_space=pltpu.SMEM)
    return pl.pallas_call(
        functools.partial(kernel, (clients, rows, width, split, groups, clusters)),
        out_shape=(
            jax.ShapeDtypeStruct((clients, clusters), f32),
            jax.ShapeDtypeStruct((1, depth // 16, width), f32),
            jax.ShapeDtypeStruct((1, depth // 16, width), f32),
        ),
        in_specs=[any_spec, any_spec, vmem_spec, smem_spec, any_spec, any_spec],
        out_specs=(vmem_spec, vmem_spec, vmem_spec),
        scratch_shapes=[
            vmem((total, depth), bf16), vmem((total, depth), bf16),
            vmem((depth, width), bf16), vmem((depth, width), bf16),
            vmem((2, grp, width), f32), vmem((2, grp, width), bf16), vmem((grp, width), bf16),
            vmem((width, total), bf16), vmem((width, total), bf16),
            vmem((8, 2, 2, width, 128), f32), vmem((8, 2, width, 128), f32),
            vmem((4, 2, split, 128), f32), vmem((2, rest, 128), f32),
            vmem((2, split, 128), f32), vmem((2, split, 128), f32), vmem((2, split, 128), f32),
            vmem((2, 2, rest, 128), f32), vmem((2, 2, rest, 128), f32), vmem((2, 2, rest, 128), f32),
            vmem((clients, 128), f32), vmem((clusters, clients, 128), f32),
            dma((2 + 2 * groups,)), dma((8, 2)), dma((8, 2)), dma((5, 2)), dma((5, 2)),
            dma((3, 3, 2)), dma((3, 3, 2)), dma((clusters,)), dma((clusters,)),
        ],
        compiler_params=pltpu.CompilerParams(
            collective_id=0, has_side_effects=True, vmem_limit_bytes=64 * 1024 * 1024 - 65536),
        name="round",
    )(user_feats, item_feats, item_ids.reshape(clients, rows), picks, user_weight, item_weight)


def solution(mesh):
    in_specs = (P("client", None), P("client", None), P("client"), P("client"),
                P("cluster", None, None), P("cluster", None, None))
    out_specs = (P("client", None), P("cluster", "client", None), P("cluster", "client", None))
    return jax.shard_map(body, mesh=mesh, in_specs=in_specs, out_specs=out_specs, check_vma=False)
```

time: 148 us -> 59.3 us (0.40)
  waiting for transfers between devices: 77.6 us -> 0 us
  Pallas kernels: 0 us -> 51.7 us
  blocking collectives: 22.6 us -> 0 us
  matrix products: 20.5 us -> 0 us
  between operations: 14.8 us -> 0.64 us
  other arithmetic: 6.34 us -> 0 us
    reduce_scatter x1 -> x0, waiting for transfers between devices: 77.6 us -> none  [body(): lax.psum_scatter(jnp.concatenate([contract_rows(user_feats, pre_slope), c...]
    pallas_call x0 -> x1, Pallas kernels: none -> 51.7 us  [body(): pl.pallas_call(functools.partial(kernel, (clients, rows, width, split, gr...]
    dot_general x7 -> x0, matrix products: 20.5 us -> none  [the longest x1 6.99 us: body(): jnp.dot(item_feats, item_map, preferred_element_type=jnp.float32)]
    all_gather x1 -> x0, blocking collectives: 16.6 us -> none  [gather_in_order(): blocks = lax.all_gather(blocks, axes[k])]
    unnamed x1 -> x0, blocking collectives: 6.02 us -> none
    concatenate x1 -> x0, other arithmetic: 3.79 us -> none  [body(): jnp.concatenate([contract_rows(user_feats, pre_slope), contract_rows(item...]
    unnamed x15 -> x3, local copies, waits for them, and re-layouts: 3.6 us -> 4.64 us
  transfers between devices with their start and end apart: 1 -> 0, of which waited for: 1 -> 0; matrix products, arithmetic and copies ran while one was open for 1% -> 0% of each run, Pallas kernels for 0% -> 0%
where the time goes in v1:
time: 59.3 us; the launch traced here: 58.4 us
  Pallas kernels  51.7 us (87%)
  local copies, waits for them, and re-layouts  6 us (10%)
  between operations  0.64 us (1%)
    pallas_call x1, Pallas kernels, body(): pl.pallas_call(functools.partial(kernel, (clients, rows, width, split, gr...  51.7 us
    unnamed x3, local copies, waits for them, and re-layouts  4.64 us
    reshape x1, local copies, waits for them, and re-layouts, body(): item_ids.reshape(clients, rows)  1.37 us

profile of v1, /device:TPU:1, one launch (start us, length us, event | category | flops | bytes accessed | tf_op | source)
XLA Modules:
  0.0 58.4 jit_solution(16542716987827760924)
XLA Ops:
  0.6 1.4 %reshape.9.ids = s32[16,96]{1,0:T(8,128)} reshape(s32[1536]{0:T(1024)} %param.8) | data formatting | bytes 12288 | tf_op jit(solution)/shard_map/reshape | solution.py:289
  2.0 51.7 %round.1 = (f32[16,16]{1,0:T(8,128)}, f32[1,128,512]{2,1,0:T(8,128)}, f32[1,128,512]{2,1,0:T(8,128)}) custom-call(bf16[1536,2048]{1,0:T(8,128)(2,1)} %uf.1, bf16[1536,2048]{1,0:T(8,128)(2,1)} %itf.1, s32[16,96]{1,0:T(8,128)} %reshape.9.ids, s32[16]{0:T(128)} %picks.1, bf16[1,2048,512]{2,1,0:T(8,128)(2,1)} %uw.1, bf16[1,2048,512]{2,1,0:T(8,128)(2,1)} %iw.1), custom_call_target="tpu_custom_call" | custom-call | tf_op jit(solution)/shard_map/round/pallas_call | solution.py:264
  53.7 1.3 %copy.12 = f32[16,16]{1,0:T(8,128)} copy(f32[16,16]{1,0:T(8,128)} %get-tuple-element.6) | data formatting | bytes 2048
  55.0 1.7 %copy.13 = f32[1,128,512]{2,1,0:T(8,128)} copy(f32[1,128,512]{2,1,0:T(8,128)} %get-tuple-element.7) | data formatting | bytes 524288
  56.7 1.7 %copy.14 = f32[1,128,512]{2,1,0:T(8,128)} copy(f32[1,128,512]{2,1,0:T(8,128)} %get-tuple-element.8) | data formatting | bytes 524288

commit v2 on v1

--- a/solution.py
+++ b/solution.py
@@ -10,12 +10,14 @@
 
 MESH = pl.DeviceIdType.MESH
 NX = 4
+VMEM_BYTES = 46 * 1024 * 1024
+AHEAD = 3
 ORDER = (2, 1, 3, 0)
 
 
-def kernel(cfg, uf, itf, ids, picks, uw, iw, loss_out, ug_out, ig_out,
-           fu, fi, wu, wi, pre, iv, uvec, pst, ist, gt, crecv, ya, yb,
-           xa1, xal, xar, xb1, xbl, xbr, tile, table,
+def kernel(cfg, uf, itf, ids_hbm, picks_hbm, uw, iw, fin, table,
+           ids, picks, fu, fi, wu, wi, pre, iv, uvec, pst, ist, gt, crecv, ya, yb,
+           xa1, xal, xar, xb1, xbl, xbr,
            ld, cs, cr, ys, yr, xs, xr, ls, lr):
     clients, rows, width, split, groups, clusters = cfg
     depth = fu.shape[1]
@@ -31,6 +33,12 @@
     across = {"client": x * 4 + (1 - y) * 2 + c}
     right = {"client": ((x + 1) % NX) * 4 + y * 2 + c}
     left = {"client": ((x + NX - 1) % NX) * 4 + y * 2 + c}
+    nz = clusters // 2
+    h = k_me // nz
+    z = k_me % nz
+    twin = {"cluster": (1 - h) * nz + z}
+    above = {"cluster": h * nz + (z + 1) % nz}
+    below = {"cluster": h * nz + (z + nz - 1) % nz}
 
     def load(src, dst, n):
         return pltpu.make_async_copy(src, dst, ld.at[n])
@@ -39,31 +47,53 @@
     load_wi = load(iw.at[0], wi, 1)
     load_u = [load(uf.at[pl.ds(g * grp, grp)], fu.at[pl.ds(g * grp, grp)], 2 + g) for g in range(groups)]
     load_i = [load(itf.at[pl.ds(g * grp, grp)], fi.at[pl.ds(g * grp, grp)], 2 + groups + g) for g in range(groups)]
-    load_wu.start()
-    load_u[0].start()
-    load_wi.start()
-    load_i[0].start()
+    load_ids = load(ids_hbm, ids, 2 + 2 * groups)
+    load_picks = load(picks_hbm, picks, 3 + 2 * groups)
+    loads = [load_wu, load_u[0], load_wi, load_i[0]]
     for g in range(1, groups):
-        load_u[g].start()
-        load_i[g].start()
+        loads += [load_u[g], load_i[g]]
+    for copy in loads[:AHEAD]:
+        copy.start()
+    load_ids.start()
+    load_picks.start()
+
+    def arrive(copy):
+        copy.wait()
+        later = [load is copy for load in loads].index(True) + AHEAD
+        if later < len(loads):
+            loads[later].start()
 
     barrier = pltpu.get_barrier_semaphore()
-    for peer in (mate, across, right, left):
+    for peer in (mate, across, right, left, twin, above, below):
         pl.semaphore_signal(barrier, inc=1, device_id=peer, device_id_type=MESH)
-    for n in range(1, clusters):
-        pl.semaphore_signal(barrier, inc=1, device_id={"cluster": (k_me + n) % clusters}, device_id_type=MESH)
-
     def towers(g):
         if g == 0:
-            load_wu.wait()
-        load_u[g].wait()
+            arrive(load_wu)
+        arrive(load_u[g])
         pre[g % 2] = jnp.dot(fu[g * grp:(g + 1) * grp, :], wu[...], preferred_element_type=jnp.float32)
         if g == 0:
-            load_wi.wait()
-        load_i[g].wait()
+            arrive(load_wi)
+        arrive(load_i[g])
         iv[g % 2] = jnp.dot(fi[g * grp:(g + 1) * grp, :], wi[...], preferred_element_type=jnp.float32).astype(jnp.bfloat16)
 
+    lane8 = lax.broadcasted_iota(jnp.int32, (8, 128), 1)
+    losses = [jnp.zeros((8, 128), jnp.float32)]
+
+    def ids_of(g, n):
+        first, off = divmod((g * per + n) * rows, 128)
+        shape = (rows, 128)
+        got = jnp.broadcast_to(ids[pl.ds(first, 1), :], shape)
+        if off:
+            got = pltpu.roll(got, 128 - off, 1)
+        if off + rows > 128:
+            more = pltpu.roll(jnp.broadcast_to(ids[pl.ds(first + 1, 1), :], shape), 128 - off, 1)
+            got = jnp.where(lax.broadcasted_iota(jnp.int32, shape, 1) < 128 - off, got, more)
+        return got[:, :rows]
+
     def slopes(g):
+        if g == 0:
+            load_ids.wait()
+            load_picks.wait()
         p = pre[g % 2]
         sig = 1.0 / (1.0 + jnp.exp(-p))
         uvec[...] = (p * sig).astype(jnp.bfloat16)
@@ -75,12 +105,12 @@
             u = uvec[at, :]
             v = iv[g % 2, at, :]
             s = lax.dot_general(u, v, (((1,), (1,)), ((), ())), preferred_element_type=jnp.float32) * temper
-            across_ids = jnp.broadcast_to(ids[pl.ds(client, 1), :], (rows, rows))
+            across_ids = ids_of(g, n)
             labels = (across_ids == across_ids.T).astype(jnp.float32)
             tail = jnp.exp(-jnp.abs(s))
             pair = jnp.maximum(s, 0.0) + jnp.log(1.0 + tail) - labels * s
             mean = jnp.sum(pair, axis=(0, 1), keepdims=True) / (rows * rows)
-            tile[pl.ds(client, 1), :] = jnp.broadcast_to(mean, (1, 128))
+            losses[0] = jnp.where(lane8 == client, mean, losses[0])
             gate = jnp.where(s >= 0.0, 1.0, tail) / (1.0 + tail)
             chosen = jnp.where(picks[client] == k_me, temper, 0.0).astype(jnp.float32)
             slope = ((gate - labels) * chosen).astype(jnp.bfloat16)
@@ -96,29 +126,46 @@
             towers(g + 1)
         slopes(g)
 
-    pl.semaphore_wait(barrier, 4 + clusters - 1)
-
-    table[pl.ds(k_me, 1)] = tile[...][None]
-    loss_copies = []
-    for n in range(1, clusters):
-        copy = pltpu.make_async_remote_copy(
-            src_ref=tile, dst_ref=table.at[k_me], send_sem=ls.at[n], recv_sem=lr.at[n],
-            device_id={"cluster": (k_me + n) % clusters}, device_id_type=MESH)
-        copy.start()
-        loss_copies.append(copy)
-
-    A = pl.ds(0, split)
-    B = pl.ds(split, width - split)
-
-    def step_of(dx, dy):
-        return 2 * ORDER.index(dx) + (1 - dy)
-
-    def own(dx, dy, t, part):
-        return gt.at[step_of(dx, dy), t, c, part]
+    pl.semaphore_wait(barrier, 7)
 
     def send(src, dst, ssem, rsem, peer):
         return pltpu.make_async_remote_copy(src_ref=src, dst_ref=dst, send_sem=ssem, recv_sem=rsem,
                                             device_id=peer, device_id_type=MESH)
+
+    table[h, z] = losses[0]
+
+    def twin_copy():
+        return send(table.at[h, z], table.at[h, z], ls.at[0], lr.at[0], twin)
+
+    def loss_copy(n, up):
+        at = (z + (nz - n if up else n)) % nz
+        part = table.at[:, pl.ds(at, 1)]
+        sem = 1 + 2 * n + (0 if up else 1)
+        return send(part, part, ls.at[sem], lr.at[sem], above if up else below)
+
+    def loss_copies(n):
+        return [loss_copy(n, True)] + ([loss_copy(n, False)] if n < nz // 2 - 1 else [])
+
+    def loss_step(n):
+        if n == 0:
+            twin_copy().wait_recv()
+        elif n <= nz // 2:
+            for copy in loss_copies(n - 1):
+                copy.wait_recv()
+        if n < nz // 2:
+            for copy in loss_copies(n):
+                copy.start()
+
+    twin_copy().start()
+
+    A = pl.ds(0, split)
+    B = pl.ds(split, width - split)
+
+    def step_of(dx, dy):
+        return 2 * ORDER.index(dx) + (1 - dy)
+
+    def own(dx, dy, t, part):
+        return gt.at[step_of(dx, dy), t, c, part]
 
     def core_copy(step, t):
         return send(gt.at[step, t, 1 - c], crecv.at[step, t], cs.at[step, t], cr.at[step, t], mate)
@@ -194,8 +241,11 @@
             @pl.when(step == n + 1)
             def _(n=n):
                 ready(n)
-                if n >= 3:
-                    far_arrived(n % 2, (n - 3) // 2)
+                if n >= 1:
+                    loss_step(n - 1)
+                if n >= 5:
+                    far_arrived(6 - n, 0)
+                    far_arrived(6 - n, 1)
         return carry
 
     lax.fori_loop(0, 2 * NX, body, 0)
@@ -215,23 +265,18 @@
     near_arrived(0)
     ya_arrived(0)
 
-    for copy in loss_copies:
-        copy.wait()
-    lane = lax.broadcasted_iota(jnp.int32, (clients, 128), 1)
-    total = jnp.zeros((clients, 128), jnp.float32)
-    for n in range(clusters):
-        total = total + jnp.where(lane == n, table[n], 0.0)
-    loss_out[...] = total[:, :clusters]
-
-    outs = (ug_out, ig_out)
     for t in (0, 1):
         yb_copy(t).wait_recv()
-        res = gt[step_of(0, 0), t, c, split:, :] + yb[t]
-        outs[t][0, :, split:] = res.T
-    near_arrived(2)
+        fin[t, split:, :] = gt[step_of(0, 0), t, c, split:, :] + yb[t]
     for t in (0, 1):
-        outs[t][0, :, :split] = gt[step_of(0, 0), t, c, :split, :].T
-
+        near_copy(2, t, True).wait_recv()
+        near_copy(2, t, False).wait_recv()
+        fin[t, :split, :] = gt[step_of(0, 0), t, c, :split, :] + xal[t] + xar[t]
+
+    twin_copy().wait_send()
+    for n in range(nz // 2):
+        for copy in loss_copies(n):
+            copy.wait_send()
     for step in range(2 * NX):
         for t in (0, 1):
             core_copy(step, t).wait_send()
@@ -243,6 +288,14 @@
             far_copy(which, t).wait_send()
             near_copy(which, t, True).wait_send()
             near_copy(which, t, False).wait_send()
+
+
+def finish(fin, table, loss_out, ug_out, ig_out):
+    clients, clusters = loss_out.shape
+    for t, out in enumerate((ug_out, ig_out)):
+        out[0] = fin[t].T
+    rows = table[...].reshape(clusters, 8, 128)[:, 0, :]
+    loss_out[...] = rows.T[:clients, :]
 
 
 def body(user_feats, item_feats, item_ids, picks, user_weight, item_weight):
@@ -258,19 +311,18 @@
     f32, bf16 = jnp.float32, jnp.bfloat16
     vmem = pltpu.VMEM
     dma = pltpu.SemaphoreType.DMA
-    any_spec = pl.BlockSpec(memory_space=pl.ANY)
+    hbm_spec = pl.BlockSpec(memory_space=pltpu.HBM)
     vmem_spec = pl.BlockSpec(memory_space=pltpu.VMEM)
-    smem_spec = pl.BlockSpec(memory_space=pltpu.SMEM)
-    return pl.pallas_call(
+    fin, table = pl.pallas_call(
         functools.partial(kernel, (clients, rows, width, split, groups, clusters)),
         out_shape=(
-            jax.ShapeDtypeStruct((clients, clusters), f32),
-            jax.ShapeDtypeStruct((1, depth // 16, width), f32),
-            jax.ShapeDtypeStruct((1, depth // 16, width), f32),
+            jax.ShapeDtypeStruct((2, width, 128), f32),
+            jax.ShapeDtypeStruct((2, clusters // 2, 8, 128), f32),
         ),
-        in_specs=[any_spec, any_spec, vmem_spec, smem_spec, any_spec, any_spec],
-        out_specs=(vmem_spec, vmem_spec, vmem_spec),
+        in_specs=[hbm_spec] * 6,
+        out_specs=(vmem_spec, vmem_spec),
         scratch_shapes=[
+            vmem((total // 128, 128), jnp.int32), pltpu.SMEM((clients,), jnp.int32),
             vmem((total, depth), bf16), vmem((total, depth), bf16),
             vmem((depth, width), bf16), vmem((depth, width), bf16),
             vmem((2, grp, width), f32), vmem((2, grp, width), bf16), vmem((grp, width), bf16),
@@ -279,14 +331,26 @@
             vmem((4, 2, split, 128), f32), vmem((2, rest, 128), f32),
             vmem((2, split, 128), f32), vmem((2, split, 128), f32), vmem((2, split, 128), f32),
             vmem((2, 2, rest, 128), f32), vmem((2, 2, rest, 128), f32), vmem((2, 2, rest, 128), f32),
-            vmem((clients, 128), f32), vmem((clusters, clients, 128), f32),
-            dma((2 + 2 * groups,)), dma((8, 2)), dma((8, 2)), dma((5, 2)), dma((5, 2)),
+            dma((4 + 2 * groups,)), dma((8, 2)), dma((8, 2)), dma((5, 2)), dma((5, 2)),
             dma((3, 3, 2)), dma((3, 3, 2)), dma((clusters,)), dma((clusters,)),
         ],
         compiler_params=pltpu.CompilerParams(
-            collective_id=0, has_side_effects=True, vmem_limit_bytes=64 * 1024 * 1024 - 65536),
+            collective_id=0, has_side_effects=True, vmem_limit_bytes=VMEM_BYTES),
         name="round",
-    )(user_feats, item_feats, item_ids.reshape(clients, rows), picks, user_weight, item_weight)
+    )(*[pltpu.with_memory_space_constraint(a, pltpu.HBM) for a in (
+        user_feats, item_feats, item_ids.reshape(total // 128, 128), picks, user_weight, item_weight)])
+    return pl.pallas_call(
+        finish,
+        out_shape=(
+            jax.ShapeDtypeStruct((clients, clusters), f32),
+            jax.ShapeDtypeStruct((1, depth // 16, width), f32),
+            jax.ShapeDtypeStruct((1, depth // 16, width), f32),
+        ),
+        in_specs=[vmem_spec, vmem_spec],
+        out_specs=(vmem_spec, vmem_spec, vmem_spec),
+        compiler_params=pltpu.CompilerParams(vmem_limit_bytes=8 * 1024 * 1024),
+        name="finish",
+    )(fin, table)
 
 
 def solution(mesh):

time: 59.3 us -> 59.3 us (level)
  the two profiles are of different devices: /device:TPU:1 before, /device:TPU:24 now
where the time goes in v2:
time: 59.3 us; the launch traced here: 59.2 us
  Pallas kernels  58.5 us (99%)
  between operations  0.64 us (1%)
    pallas_call x1, Pallas kernels, body(): pl.pallas_call(functools.partial(kernel, (clients, rows, width, split, gr...  57.6 us

profile of v2, /device:TPU:24, one launch (start us, length us, event | category | flops | bytes accessed | tf_op | source)
XLA Modules:
  0.0 59.2 jit_solution(12879664494780384182)
XLA Ops:
  0.6 57.6 %round.1 = (f32[2,512,128]{2,1,0:T(8,128)S(1)}, f32[2,8,8,128]{3,2,1,0:T(8,128)S(1)}) custom-call(bf16[1536,2048]{1,0:T(8,128)(2,1)} %uf.1, bf16[1536,2048]{1,0:T(8,128)(2,1)} %itf.1, s32[12,128]{1,0:T(8,128)} %bitcast.1, s32[16]{0:T(128)} %picks_hbm.1, bf16[1,2048,512]{2,1,0:T(8,128)(2,1)} %uw.1, bf16[1,2048,512]{2,1,0:T(8,128)(2,1)} %iw.1), custom_call_target="tpu_custom_call" | custom-call | tf_op jit(solution)/shard_map/round/pallas_call | solution.py:316
  58.3 0.9 %finish.1 = (f32[16,16]{1,0:T(8,128)}, f32[1,128,512]{2,1,0:T(8,128)}, f32[1,128,512]{2,1,0:T(8,128)}) custom-call(f32[2,512,128]{2,1,0:T(8,128)S(1)} %get-tuple-element.5.fin, f32[2,8,8,128]{3,2,1,0:T(8,128)S(1)} %get-tuple-element.6.table), custom_call_target="tpu_custom_call" | custom-call | tf_op jit(solution)/shard_map/finish/pallas_call | solution.py:342
